TPU v7x, 32 devices: a whole 2x2x4 slice. The times are simulated.
32 devices in a mesh: req: 8 (over z, x), grp: 4 (over y, core).
Axes of the slice: x: 2, y: 2, z: 4, core: 2. Of those that a mesh axis runs over, the one named last changes fastest.
Arguments:
- hidden: bfloat16 [256, 16, 1024], P(('grp', 'req')), parts along dimension 0, may hold values from -6 to 6
- norm_gain: float32 [1024], replicated, may hold values from 0.1 to 1.9
- in_weight: bfloat16 [1024, 4096], replicated, may hold values from -0.1875 to 0.1875
- conv_weight: float32 [4, 2048], P(None, 'req'), may hold values from -3 to 3
- conv_bias: float32 [2048], P('req'), may hold values from -3 to 3
- x_weight: bfloat16 [2048, 160], P('req'), may hold values from -0.125 to 0.125
- step_weight: bfloat16 [128, 2048], P(None, 'req'), may hold values from -0.5 to 0.5
- step_bias: float32 [2048], P('req'), may hold values from -5 to -1
- log_decay: float32 [16, 2048], P(None, 'req'), may hold values from -0.7 to 2.8
- skip_gain: float32 [2048], P('req'), may hold values from 0.5 to 1.5
- out_weight: bfloat16 [2048, 1024], replicated, may hold values from -0.125 to 0.125
- old_states: float32 [256, 16, 2048], P(('grp', 'req')), parts along dimension 0, may hold values from -3 to 3
- old_edges: bfloat16 [256, 3, 2048], P(('grp', 'req')), parts along dimension 0, may hold values from -6 to 6
- anchor: int32 [256], P('grp'), parts along dimension 0, may hold values from 0 to 63, each once
- fresh_flag: int32 [256], P('grp'), parts along dimension 0, may hold values 0 or 1
- accepted: int32 [256], P('grp'), parts along dimension 0, may hold values from 1 to 16
- request_ages: int32 [256], P('grp'), parts along dimension 0, may hold values from 0 to 7
Outputs:
- layer_out: bfloat16 [256, 16, 1024], P(('grp', 'req')), parts along dimension 0
- new_states: float32 [256, 16, 2048], P(('grp', 'req')), parts along dimension 0
There are 4 independent parts, one for each index of `grp`. A program takes and returns all parts, laid end to end along the dimension named above; an argument that names none is the same for every part. Nothing has to cross between parts.
Inputs may be any that keep to these rules, and one draw needn't show every extreme that they name: Every old slot is the anchor of exactly one request.
All inputs are finite; a program needn't handle non-finite values.
Results may differ from a plain program's by a relative error of at most 0.0091.
Values may be sent and summed in bfloat16 or wider, within the bound.
No kernel may reach another device: no remote copies, remote signals or barrier semaphores. Data moves between devices by JAX's collectives and lax.ppermute only.
A program may use at most 128 MiB of HBM per device.

v0:
```python
import jax
import jax.numpy as jnp
from jax import lax
from jax.sharding import PartitionSpec as P

EPS = 1e-05


def rms_normed(values_in, norm_gain):
    values = values_in.astype(jnp.float32)
    factor = lax.rsqrt(jnp.mean(values * values, axis=-1, keepdims=True) + EPS)
    return (values * factor * norm_gain).astype(jnp.bfloat16)


def on_device(
    hidden,
    norm_gain,
    in_weight,
    conv_weight,
    conv_bias,
    x_weight,
    step_weight,
    step_bias,
    log_decay,
    skip_gain,
    out_weight,
    old_states,
    old_edges,
    anchor,
    fresh_flag,
    accepted,
    request_ages,
):
    local_reqs, draft_len, width = hidden.shape
    inner_width = out_weight.shape[0]
    channels = conv_weight.shape[1]
    state_size = log_decay.shape[0]
    low_rank = step_weight.shape[0]
    span = old_edges.shape[1]
    state_lead = jnp.swapaxes(old_states, 0, 1)
    edge_lead = jnp.swapaxes(old_edges.astype(jnp.float32), 0, 1)
    moved_states, moved_edges = (
        lax.all_to_all(state_lead, "req", split_axis=2, concat_axis=1, tiled=True),
        lax.all_to_all(edge_lead, "req", split_axis=2, concat_axis=1, tiled=True),
    )
    token_major = jnp.swapaxes(hidden, 0, 1).reshape(draft_len * local_reqs, width)
    normed = rms_normed(token_major, norm_gain)
    projected = jnp.dot(normed, in_weight, preferred_element_type=jnp.float32).astype(jnp.bfloat16)
    projected = jnp.moveaxis(projected.reshape(draft_len, local_reqs, 2, inner_width), 2, 0)
    grouped = lax.all_to_all(projected, "req", split_axis=3, concat_axis=2, tiled=True)
    all_reqs = grouped.shape[2]
    inner_part = grouped[0]
    gate_part = grouped[1]
    keep_state = (1 - fresh_flag).astype(jnp.float32)
    start_state = jnp.take(moved_states, anchor, axis=1) * keep_state[None, :, None]
    edges = jnp.take(moved_edges, anchor, axis=1)
    distance = span - jnp.arange(span, dtype=jnp.int32)
    usable = (distance[:, None] <= request_ages[None, :]) & (fresh_flag[None, :] == 0)
    history = jnp.where(usable[:, :, None], edges, jnp.zeros((), jnp.float32))
    sequence = jnp.concatenate([history, inner_part.astype(jnp.float32)], axis=0)
    running = conv_bias + conv_weight[0] * sequence[0:draft_len]
    for offset in range(1, conv_weight.shape[0]):
        running = running + conv_weight[offset] * sequence[offset : offset + draft_len]
    conv_out = jax.nn.silu(running).astype(jnp.bfloat16)
    conv_rows = conv_out.reshape(draft_len * all_reqs, channels)
    partial_value = jnp.dot(conv_rows, x_weight, preferred_element_type=jnp.float32)
    mixed_rows = lax.psum(partial_value, "req").astype(jnp.bfloat16)
    flat = all_reqs * channels
    step_sizes = jax.nn.softplus(
        jnp.dot(mixed_rows[:, :low_rank], step_weight, preferred_element_type=jnp.float32)
        + step_bias
    )
    step_sizes = step_sizes.reshape(draft_len, flat)
    coeffs = (
        mixed_rows[:, low_rank:].astype(jnp.float32).reshape(draft_len, all_reqs, 2 * state_size)
    )
    b_coeff = coeffs[:, :, :state_size]
    c_coeff = coeffs[:, :, state_size:]
    inputs = conv_out.astype(jnp.float32)
    flat_inputs = inputs.reshape(draft_len, flat)
    decay = jnp.broadcast_to(
        (-jnp.exp(log_decay))[:, None, :], (state_size, all_reqs, channels)
    ).reshape(state_size, flat)
    start_flat = start_state.reshape(state_size, flat)

    def spread(per_token):
        return jnp.broadcast_to(
            jnp.swapaxes(per_token, 0, 1)[:, :, None], (state_size, all_reqs, channels)
        ).reshape(state_size, flat)

    def advance(carried, sliced):
        current, chosen = carried
        step_delta, step_b, step_c, step_input, step_index = sliced
        factor = jnp.exp(step_delta[None, :] * decay)
        current = factor * current + (step_delta * step_input)[None, :] * spread(step_b)
        result = jnp.sum(spread(step_c) * current, axis=0)
        picked = jnp.broadcast_to(
            (accepted == step_index + 1)[:, None], (all_reqs, channels)
        ).reshape(flat)
        chosen = jnp.where(picked[None, :], current, chosen)
        return ((current, chosen), result)

    sliced = (step_sizes, b_coeff, c_coeff, flat_inputs, jnp.arange(draft_len, dtype=jnp.int32))
    (final_state, chosen), outputs = lax.scan(advance, (start_flat, start_flat), sliced)
    outputs = outputs.reshape(draft_len, all_reqs, channels)
    gated_rows = (
        (outputs + skip_gain * inputs) * jax.nn.silu(gate_part.astype(jnp.float32))
    ).astype(jnp.bfloat16)
    returned = lax.all_to_all(gated_rows, "req", split_axis=1, concat_axis=2, tiled=True)
    layer_out = jnp.dot(
        returned.reshape(draft_len * local_reqs, inner_width),
        out_weight,
        preferred_element_type=jnp.float32,
    ).astype(jnp.bfloat16)
    layer_out = jnp.swapaxes(layer_out.reshape(draft_len, local_reqs, width), 0, 1)
    owned = lax.all_to_all(
        chosen.reshape(state_size, all_reqs, channels),
        "req",
        split_axis=1,
        concat_axis=2,
        tiled=True,
    )
    return (layer_out, jnp.swapaxes(owned, 0, 1))


def solution(mesh):
    return jax.shard_map(
        on_device,
        mesh=mesh,
        in_specs=(
            P(("grp", "req"), None, None),
            P(),
            P(),
            P(None, "req"),
            P("req"),
            P("req", None),
            P(None, "req"),
            P("req"),
            P(None, "req"),
            P("req"),
            P(),
            P(("grp", "req"), None, None),
            P(("grp", "req"), None, None),
            P("grp"),
            P("grp"),
            P("grp"),
            P("grp"),
        ),
        out_specs=(P(("grp", "req"), None, None), P(("grp", "req"), None, None)),
        check_vma=False,
    )
```

profile of v0, /device:TPU:0, one launch (start us, length us, event | category | flops | bytes accessed | tf_op | source)
XLA Modules:
  0.0 369.8 jit_solution(14479661632174473123)
XLA Ops:
  0.7 4.0 %copy.100 = f32[8,3,2048]{0,1,2:T(4,128)} copy(bf16[8,3,2048]{2,0,1:T(8,128)(2,1)} %param.31) | data formatting | bytes 294912 | tf_op jit(solution)/shard_map/transpose | solution.py:41
  4.7 3.9 %bitcast_bitcast_fusion.2 = f32[2048,3,8]{2,1,0:T(4,128)} fusion(f32[8,3,2048]{0,1,2:T(4,128)} %copy.100), kind=kLoop, calls=%fused_computation.72 | loop fusion | bytes 393216
  8.6 5.1 %reshape.188 = f32[8,1,6144]{2,1,0:T(1,128)} reshape(f32[2048,3,8]{2,1,0:T(4,128)} %bitcast_bitcast_fusion.2) | data formatting | bytes 393216
  13.7 7.3 %all-to-all-start.1 = ((f32[8,1,6144]{2,1,0:T(1,128)}), f32[8,1,6144]{2,1,0:T(1,128)S(1)}, u32[]{:S(2)}, u32[]{:S(2)}) async-start(f32[8,1,6144]{2,1,0:T(1,128)} %reshape.188), calls=%async_computation.1 | async-start | bytes 393216 | tf_op jit(solution)/shard_map/all_to_all | solution.py:44
  20.9 4.7 %copy.94 = f32[8,16,2048]{1,0,2:T(8,128)} copy(f32[8,16,2048]{2,1,0:T(8,128)S(1)} %copy-done.3) | data formatting | bytes 2097152 | tf_op args[11]
  26.0 4.8 %convolution_convert_fusion = bf16[128,4096]{1,0:T(8,128)(2,1)S(1)} fusion(bf16[1024,4096]{1,0:T(8,128)(2,1)} %param.21, f32[1024]{0:T(1024)S(1)} %copy-done.4, f32[128]{0:T(128)S(1)} %rsqrt.12, bf16[8,16,1024]{2,1,0:T(8,128)(2,1)S(1)} %copy-done.2), kind=kOutput, calls=%fused_computation.11 | convolution fusion | flops 1074790400 | bytes 9703936 | tf_op jit(solution)/shard_map/dot_general | solution.py:48
  30.8 8.9 %copy.103 = bf16[16,8,2,2048]{0,1,2,3:T(8,128)(2,1)} copy(bf16[16,8,2,2048]{3,1,2,0:T(8,128)(2,1)S(1)} %bitcast.169) | data formatting | bytes 2097152 | tf_op jit(solution)/shard_map/reshape | solution.py:49
  39.6 7.5 %bitcast_bitcast_fusion = bf16[2048,2,8,16]{3,2,1,0:T(8,128)(2,1)} fusion(bf16[16,8,2,2048]{0,1,2,3:T(8,128)(2,1)} %copy.103), kind=kLoop, calls=%fused_computation.70 | loop fusion | bytes 2097152
  47.1 5.8 %bitcast_bitcast_fusion.1 = f32[2048,8,16]{2,1,0:T(8,128)} fusion(f32[8,16,2048]{1,0,2:T(8,128)} %copy.94), kind=kLoop, calls=%fused_computation.71 | loop fusion | bytes 2097152
  52.9 8.1 %reshape.184 = f32[8,1,32768]{2,1,0:T(1,128)} reshape(f32[2048,8,16]{2,1,0:T(8,128)} %bitcast_bitcast_fusion.1) | data formatting | bytes 2097152
  61.1 6.0 %all-to-all-start = ((f32[8,1,32768]{2,1,0:T(1,128)}), f32[8,1,32768]{2,1,0:T(1,128)S(1)}, u32[]{:S(2)}, u32[]{:S(2)}) async-start(f32[8,1,32768]{2,1,0:T(1,128)} %reshape.184), calls=%async_computation | async-start | bytes 2097152 | tf_op jit(solution)/shard_map/all_to_all | solution.py:43
  67.3 11.3 %reshape.186 = bf16[8,2,32768]{2,1,0:T(2,128)(2,1)} reshape(bf16[2048,2,8,16]{3,2,1,0:T(8,128)(2,1)} %bitcast_bitcast_fusion) | data formatting | bytes 2097152
  80.5 4.7 %reshape.189 = f32[2048,3,8]{2,1,0:T(4,128)} reshape(f32[8,6144]{1,0:T(8,128)S(1)} %reduce.3) | data formatting | bytes 393216
  85.2 3.5 copy.101
  89.6 2.9 all-to-all-done
  92.5 3.7 %all-to-all-start.2 = ((bf16[8,2,32768]{2,1,0:T(2,128)(2,1)}), bf16[8,2,32768]{2,1,0:T(2,128)(2,1)S(1)}, u32[]{:S(2)}, u32[]{:S(2)}) async-start(bf16[8,2,32768]{2,1,0:T(2,128)(2,1)} %reshape.186), calls=%async_computation.2 | async-start | bytes 2097152 | tf_op jit(solution)/shard_map/all_to_all | solution.py:50
  96.3 3.1 reduce.2
  99.4 6.1 %reshape.185 = f32[2048,8,16]{2,1,0:T(8,128)} reshape(f32[8,32768]{1,0:T(8,128)S(1)} %reduce.2) | data formatting | bytes 2097152
  105.5 5.4 %copy.96 = f32[16,8,8,256]{3,2,1,0:T(8,128)S(1)} copy(f32[16,8,8,256]{0,2,3,1:T(8,128)} %bitcast.155) | data formatting | bytes 2097152 | tf_op jit(solution)/shard_map/all_to_all | solution.py:43
  112.4 9.5 %all-to-all-done.2 = bf16[8,2,32768]{2,1,0:T(2,128)(2,1)S(1)} async-done(((bf16[8,2,32768]{2,1,0:T(2,128)(2,1)}), bf16[8,2,32768]{2,1,0:T(2,128)(2,1)S(1)}, u32[]{:S(2)}, u32[]{:S(2)}) %all-to-all-start.2) | async-done | bytes 1048608 | tf_op jit(solution)/shard_map/all_to_all | solution.py:50
  121.9 7.6 %reshape.187 = bf16[2048,2,8,16]{3,2,1,0:T(8,128)(2,1)} reshape(bf16[8,2,32768]{2,1,0:T(2,128)(2,1)S(1)} %all-to-all-done.2) | data formatting | bytes 2097152
  129.5 8.9 %copy.104 = bf16[2,16,8,8,256]{4,2,3,1,0:T(8,128)(2,1)S(1)} copy(bf16[2,16,8,8,256]{1,2,0,4,3:T(8,128)(2,1)} %bitcast.156) | data formatting | bytes 2097152 | tf_op jit(solution)/shard_map/all_to_all | solution.py:50
  140.2 43.6 %all-reduce.1 = bf16[1024,160]{0,1:T(8,128)(2,1)} all-reduce(f32[1024,160]{0,1:T(8,128)S(1)} %fusion.29), channel_id=1, replica_groups=mesh['req'=8,'grp'=4] {'req'}, use_global_device_ids=true, to_apply=%region_1.2 | all-reduce | flops 163840 | bytes 983040 | tf_op jit(solution)/shard_map/psum | solution.py:67
  184.7 2.7 compare_select_fusion
  187.4 2.4 reshape.145
  191.2 132.7 %while.15 = (s32[]{:T(128)}, f32[16,16384]{1,0:T(8,128)S(1)}, f32[16,16384]{1,0:T(8,128)S(1)}, f32[16,16384]{1,0:T(8,128)}, f32[16,16384]{1,0:T(8,128)}, /*index...) while((s32[]{:T(128)}, f32[16,16384]{1,0:T(8,128)S(1)}, ...), condition=%wide.region_4.5_spmd.clone, body=%wide.region_2.4_spmd.clone.sunk | while | flops 1835075 | bytes 18522676 | solution.py:104
  197.6 1.9 dynamic_update_slice.6
  205.9 1.9 dynamic_update_slice.6
  214.2 1.9 dynamic_update_slice.6
  222.5 1.9 dynamic_update_slice.6
  230.7 1.9 dynamic_update_slice.6
  239.0 1.9 dynamic_update_slice.6
  247.3 1.9 dynamic_update_slice.6
  255.6 1.9 dynamic_update_slice.6
  263.9 1.9 dynamic_update_slice.6
  272.2 1.9 dynamic_update_slice.6
  280.5 1.9 dynamic_update_slice.6
  288.8 1.9 dynamic_update_slice.6
  297.1 1.9 dynamic_update_slice.6
  305.4 1.9 dynamic_update_slice.6
  313.7 1.9 dynamic_update_slice.6
  322.0 1.9 dynamic_update_slice.6
  328.1 3.5 all-to-all-start.3
  332.7 9.4 %all-to-all-done.3 = bf16[16,64,256]{2,0,1:T(8,128)(2,1)S(1)} async-done(((bf16[16,64,256]{2,0,1:T(8,128)(2,1)}), bf16[16,64,256]{2,0,1:T(8,128)(2,1)S(1)}, u32[]{:S(2)}, u32[]{:S(2)}) %all-to-all-start.3) | async-done | bytes 524320 | tf_op jit(solution)/shard_map/all_to_all | solution.py:109
  342.1 9.1 %all-to-all-start.4 = ((f32[16,64,256]{2,0,1:T(8,128)}), f32[16,64,256]{2,0,1:T(8,128)S(1)}, u32[]{:S(2)}, u32[]{:S(2)}) async-start(f32[16,64,256]{2,0,1:T(8,128)} %bitcast.121), calls=%async_computation.4 | async-start | bytes 2097152 | tf_op jit(solution)/shard_map/all_to_all | solution.py:116
  351.6 2.9 fusion.2
  355.4 12.2 %all-to-all-done.4 = f32[16,64,256]{2,0,1:T(8,128)S(1)} async-done(((f32[16,64,256]{2,0,1:T(8,128)}), f32[16,64,256]{2,0,1:T(8,128)S(1)}, u32[]{:S(2)}, u32[]{:S(2)}) %all-to-all-start.4) | async-done | bytes 1048608 | tf_op jit(solution)/shard_map/all_to_all | solution.py:116
  368.2 1.6 copy.113
  (299 shorter events, 105.4 us)
Async XLA Ops:
  0.6 139.3 %copy-start = (bf16[256,160]{0,1:T(8,128)(2,1)S(1)}, bf16[256,160]{0,1:T(8,128)(2,1)}, u32[]{:S(2)}) copy-start(bf16[256,160]{0,1:T(8,128)(2,1)} %param.24) | copy-start | bytes 245764
  0.6 20.3 %copy-start.3 = (f32[8,16,2048]{2,1,0:T(8,128)S(1)}, f32[8,16,2048]{2,1,0:T(8,128)}, u32[]{:S(2)}) copy-start(f32[8,16,2048]{2,1,0:T(8,128)} %param.30) | copy-start | bytes 3145732
  8.6 17.1 %copy-start.2 = (bf16[8,16,1024]{2,1,0:T(8,128)(2,1)S(1)}, bf16[8,16,1024]{2,1,0:T(8,128)(2,1)}, u32[]{:S(2)}) copy-start(bf16[8,16,1024]{2,1,0:T(8,128)(2,1)} %param.19) | copy-start | bytes 786436
  8.6 17.4 %copy-start.4 = (f32[1024]{0:T(1024)S(1)}, f32[1024]{0:T(1024)}, u32[]{:S(2)}) copy-start(f32[1024]{0:T(1024)} %param.20) | copy-start | bytes 12292
  13.7 47.4 %all-to-all-start.1 = ((f32[8,1,6144]{2,1,0:T(1,128)}), f32[8,1,6144]{2,1,0:T(1,128)S(1)}, u32[]{:S(2)}, u32[]{:S(2)}) async-start(f32[8,1,6144]{2,1,0:T(1,128)} %reshape.188), calls=%async_computation.1 | async-start | bytes 393216 | tf_op jit(solution)/shard_map/all_to_all | solution.py:44
  52.9 8.2 %copy-start.12 = (s32[64]{0:T(128)S(1)}, s32[64]{0:T(128)}, u32[]{:S(2)}) copy-start(s32[64]{0:T(128)} %param.33) | copy-start | bytes 772
  52.9 14.3 %copy-start.13 = (s32[64]{0:T(128)S(1)}, s32[64]{0:T(128)}, u32[]{:S(2)}) copy-start(s32[64]{0:T(128)} %param.32) | copy-start | bytes 772
  52.9 25.7 %copy-start.9 = (s32[64]{0:T(128)S(1)}, s32[64]{0:T(128)}, u32[]{:S(2)}) copy-start(s32[64]{0:T(128)} %param.35) | copy-start | bytes 772
  52.9 25.9 %copy-start.6 = (f32[4,256]{1,0:T(4,128)S(1)}, f32[4,256]{1,0:T(4,128)}, u32[]{:S(2)}) copy-start(f32[4,256]{1,0:T(4,128)} %param.22) | copy-start | bytes 12292
  52.9 25.9 %copy-start.5 = (f32[16,256]{1,0:T(8,128)S(1)}, f32[16,256]{1,0:T(8,128)}, u32[]{:S(2)}) copy-start(f32[16,256]{1,0:T(8,128)} %param.27) | copy-start | bytes 49156
  61.1 31.4 %all-to-all-start = ((f32[8,1,32768]{2,1,0:T(1,128)}), f32[8,1,32768]{2,1,0:T(1,128)S(1)}, u32[]{:S(2)}, u32[]{:S(2)}) async-start(f32[8,1,32768]{2,1,0:T(1,128)} %reshape.184), calls=%async_computation | async-start | bytes 2097152 | tf_op jit(solution)/shard_map/all_to_all | solution.py:43
  92.5 29.4 %all-to-all-start.2 = ((bf16[8,2,32768]{2,1,0:T(2,128)(2,1)}), bf16[8,2,32768]{2,1,0:T(2,128)(2,1)S(1)}, u32[]{:S(2)}, u32[]{:S(2)}) async-start(bf16[8,2,32768]{2,1,0:T(2,128)(2,1)} %reshape.186), calls=%async_computation.2 | async-start | bytes 2097152 | tf_op jit(solution)/shard_map/all_to_all | solution.py:50
  112.4 27.0 %copy-start.7 = (f32[256]{0:T(256)S(1)}, f32[256]{0:T(256)}, u32[]{:S(2)}) copy-start(f32[256]{0:T(256)} %param.23) | copy-start | bytes 3076
  129.5 55.2 %copy-start.10 = (bf16[128,256]{1,0:T(8,128)(2,1)S(1)}, bf16[128,256]{1,0:T(8,128)(2,1)}, u32[]{:S(2)}) copy-start(bf16[128,256]{1,0:T(8,128)(2,1)} %param.25) | copy-start | bytes 196612
  129.5 55.2 %copy-start.11 = (f32[256]{0:T(256)S(1)}, f32[256]{0:T(256)}, u32[]{:S(2)}) copy-start(f32[256]{0:T(256)} %param.26) | copy-start | bytes 3076
  138.4 1.0 copy-start.1
  138.4 52.8 %copy-start.14 = (s32[64]{0:T(128)S(1)}, s32[64]{0:T(128)}, u32[]{:S(2)}) copy-start(s32[64]{0:T(128)} %param.34) | copy-start | bytes 772
  191.2 134.3 %copy-start.8 = (f32[256]{0:T(256)S(1)}, f32[256]{0:T(256)}, u32[]{:S(2)}) copy-start(f32[256]{0:T(256)} %param.28) | copy-start | bytes 3076
  328.1 14.0 %all-to-all-start.3 = ((bf16[16,64,256]{2,0,1:T(8,128)(2,1)}), bf16[16,64,256]{2,0,1:T(8,128)(2,1)S(1)}, u32[]{:S(2)}, u32[]{:S(2)}) async-start(bf16[16,64,256]{2,0,1:T(8,128)(2,1)} %copy.108), calls=%async_computation.3 | async-start | bytes 1048576 | tf_op jit(solution)/shard_map/all_to_all | solution.py:109
  342.1 25.5 %all-to-all-start.4 = ((f32[16,64,256]{2,0,1:T(8,128)}), f32[16,64,256]{2,0,1:T(8,128)S(1)}, u32[]{:S(2)}, u32[]{:S(2)}) async-start(f32[16,64,256]{2,0,1:T(8,128)} %bitcast.121), calls=%async_computation.4 | async-start | bytes 2097152 | tf_op jit(solution)/shard_map/all_to_all | solution.py:116
where the time goes:
time: 372 us; the launch traced here: 370 us
  local copies, waits for them, and re-layouts  191 us (51%)
  other arithmetic  47.8 us (13%)
  blocking collectives  43.6 us (12%)
  waiting for transfers between devices  33.9 us (9%)
  starting transfers between devices  29.5 us (8%)
  loops' own time  12.3 us (3%)
  matrix products  10.8 us (3%)
    unnamed x47, local copies, waits for them, and re-layouts  70.4 us
    psum x1, blocking collectives, on_device(): mixed_rows = lax.psum(partial_value, 'req').astype(jnp.bfloat16)  43.6 us
    dynamic_update_slice x16, local copies, waits for them, and re-layouts, on_device(): lax.scan(advance, (start_flat, start_flat), sliced)  31.1 us
    while x48, local copies, waits for them, and re-layouts  29.4 us
    dynamic_slice x16, other arithmetic, on_device(): lax.scan(advance, (start_flat, start_flat), sliced)  20.9 us
    reduce_sum x16, other arithmetic, advance(): result = jnp.sum(spread(step_c) * current, axis=0)  14.9 us
    another operation x1, loops' own time, on_device(): lax.scan(advance, (start_flat, start_flat), sliced)  12.3 us
    all_to_all x1, waiting for transfers between devices, on_device(): lax.all_to_all(chosen.reshape(state_size, all_reqs, channels), 'req', spl...  12.2 us
  transfers between devices with their start and end apart: 5, of which 4 were waited for; matrix products, arithmetic and copies ran while one was open for 23% of the time, Pallas kernels for 0%

commit v1 on v0

--- a/solution.py
+++ b/solution.py
@@ -40,7 +40,12 @@
     state_lead = jnp.swapaxes(old_states, 0, 1)
     edge_lead = jnp.swapaxes(old_edges.astype(jnp.float32), 0, 1)
     moved_states, moved_edges = (
-        lax.all_to_all(state_lead, "req", split_axis=2, concat_axis=1, tiled=True),
+        jnp.concatenate(
+            lax.all_to_all(
+                jnp.stack(jnp.split(state_lead, lax.axis_size("req"), axis=2)), "req", 0, 0
+            ),
+            axis=1,
+        ),
         lax.all_to_all(edge_lead, "req", split_axis=2, concat_axis=1, tiled=True),
     )
     token_major = jnp.swapaxes(hidden, 0, 1).reshape(draft_len * local_reqs, width)

time: 372 us -> 350 us (0.941)
  local copies, waits for them, and re-layouts: 191 us -> 164 us
  waiting for transfers between devices: 33.9 us -> 47.5 us
    unnamed x47 -> x52, local copies, waits for them, and re-layouts: 70.4 us -> 50.3 us
    all_to_all x1, waiting for transfers between devices: 9.5 us -> 23.9 us  [on_device(): lax.all_to_all(projected, 'req', split_axis=3, concat_axis=2, tiled=True)]
    all_to_all x3 -> x0, local copies, waits for them, and re-layouts: 6.51 us -> none  [on_device(): lax.all_to_all(state_lead, 'req', split_axis=2, concat_axis=1, tiled=True)]
    all_to_all x1, starting transfers between devices: 9.06 us -> 3.78 us  [on_device(): lax.all_to_all(chosen.reshape(state_size, all_reqs, channels), 'req', spl...]
  transfers between devices with their start and end apart: 5 -> 5, of which waited for: 4 -> 3; matrix products, arithmetic and copies ran while one was open for 23% -> 16% of each run, Pallas kernels for 0% -> 0%
where the time goes in v1:
time: 350 us; the launch traced here: 348 us
  local copies, waits for them, and re-layouts  164 us (47%)
  waiting for transfers between devices  47.5 us (14%)
  other arithmetic  44.6 us (13%)
  blocking collectives  43.3 us (12%)
  starting transfers between devices  26.5 us (8%)
  matrix products  10.8 us (3%)
  loops' own time  10.3 us (3%)
    unnamed x52, local copies, waits for them, and re-layouts  50.3 us
    psum x1, blocking collectives, on_device(): mixed_rows = lax.psum(partial_value, 'req').astype(jnp.bfloat16)  43.3 us
    dynamic_update_slice x16, local copies, waits for them, and re-layouts, on_device(): lax.scan(advance, (start_flat, start_flat), sliced)  31.3 us
    while x48, local copies, waits for them, and re-layouts  29.4 us
    all_to_all x1, waiting for transfers between devices, on_device(): lax.all_to_all(projected, 'req', split_axis=3, concat_axis=2, tiled=True)  23.9 us
    dynamic_slice x16, other arithmetic, on_device(): lax.scan(advance, (start_flat, start_flat), sliced)  20.9 us
    reduce_sum x16, other arithmetic, advance(): result = jnp.sum(spread(step_c) * current, axis=0)  14.9 us
    all_to_all x1, waiting for transfers between devices, on_device(): lax.all_to_all(chosen.reshape(state_size, all_reqs, channels), 'req', spl...  14.4 us
  transfers between devices with their start and end apart: 5, of which 3 were waited for; matrix products, arithmetic and copies ran while one was open for 16% of the time, Pallas kernels for 0%

profile of v1, /device:TPU:0, one launch (start us, length us, event | category | flops | bytes accessed | tf_op | source)
XLA Modules:
  0.0 348.0 jit_solution(10017953270379130450)
XLA Ops:
  0.6 3.9 %copy.80 = f32[8,3,2048]{0,1,2:T(4,128)} copy(bf16[8,3,2048]{2,0,1:T(8,128)(2,1)} %param.31) | data formatting | bytes 294912 | tf_op jit(solution)/shard_map/transpose | solution.py:41
  4.6 3.9 %bitcast_bitcast_fusion.1 = f32[2048,3,8]{2,1,0:T(4,128)} fusion(f32[8,3,2048]{0,1,2:T(4,128)} %copy.80), kind=kLoop, calls=%fused_computation.87 | loop fusion | bytes 393216
  8.5 5.2 %reshape.194 = f32[8,1,6144]{2,1,0:T(1,128)} reshape(f32[2048,3,8]{2,1,0:T(4,128)} %bitcast_bitcast_fusion.1) | data formatting | bytes 393216
  13.7 7.3 %all-to-all-start.1 = ((f32[8,1,6144]{2,1,0:T(1,128)}), f32[8,1,6144]{2,1,0:T(1,128)S(1)}, u32[]{:S(2)}, u32[]{:S(2)}) async-start(f32[8,1,6144]{2,1,0:T(1,128)} %reshape.194), calls=%async_computation.1 | async-start | bytes 393216 | tf_op jit(solution)/shard_map/all_to_all | solution.py:49
  26.2 4.8 %convolution_convert_fusion = bf16[128,4096]{1,0:T(8,128)(2,1)S(1)} fusion(bf16[1024,4096]{1,0:T(8,128)(2,1)} %param.21, f32[1024]{0:T(1024)S(1)} %copy-done.5, f32[128]{0:T(128)S(1)} %rsqrt.12, bf16[8,16,1024]{2,1,0:T(8,128)(2,1)S(1)} %copy-done.3), kind=kOutput, calls=%fused_computation.11 | convolution fusion | flops 1074790400 | bytes 9703936 | tf_op jit(solution)/shard_map/dot_general | solution.py:53
  31.2 8.8 %copy.83 = bf16[16,8,2,2048]{0,1,2,3:T(8,128)(2,1)} copy(bf16[16,8,2,2048]{3,1,2,0:T(8,128)(2,1)S(1)} %bitcast.194) | data formatting | bytes 2097152 | tf_op jit(solution)/shard_map/reshape | solution.py:54
  40.7 6.0 %all-to-all-start = ((f32[8,16,8,256]{3,1,2,0:T(8,128)}), f32[8,16,8,256]{3,1,2,0:T(8,128)S(1)}, u32[]{:S(2)}, u32[]{:S(2)}) async-start(f32[8,16,8,256]{3,1,2,0:T(8,128)} %fusion.27), calls=%async_computation | async-start | bytes 2097152 | tf_op jit(solution)/shard_map/all_to_all | solution.py:44
  46.7 7.5 %bitcast_bitcast_fusion = bf16[2048,2,8,16]{3,2,1,0:T(8,128)(2,1)} fusion(bf16[16,8,2,2048]{0,1,2,3:T(8,128)(2,1)} %copy.83), kind=kLoop, calls=%fused_computation.86 | loop fusion | bytes 2097152
  54.2 11.3 %reshape.192 = bf16[8,2,32768]{2,1,0:T(2,128)(2,1)} reshape(bf16[2048,2,8,16]{3,2,1,0:T(8,128)(2,1)} %bitcast_bitcast_fusion) | data formatting | bytes 2097152
  67.0 4.7 %reshape.195 = f32[2048,3,8]{2,1,0:T(4,128)} reshape(f32[8,6144]{1,0:T(8,128)S(1)} %reduce.2) | data formatting | bytes 393216
  71.7 3.5 copy.81
  76.2 6.0 %all-to-all-start.2 = ((bf16[8,2,32768]{2,1,0:T(2,128)(2,1)}), bf16[8,2,32768]{2,1,0:T(2,128)(2,1)S(1)}, u32[]{:S(2)}, u32[]{:S(2)}) async-start(bf16[8,2,32768]{2,1,0:T(2,128)(2,1)} %reshape.192), calls=%async_computation.2 | async-start | bytes 2097152 | tf_op jit(solution)/shard_map/all_to_all | solution.py:55
  83.1 23.9 %all-to-all-done.2 = bf16[8,2,32768]{2,1,0:T(2,128)(2,1)S(1)} async-done(((bf16[8,2,32768]{2,1,0:T(2,128)(2,1)}), bf16[8,2,32768]{2,1,0:T(2,128)(2,1)S(1)}, u32[]{:S(2)}, u32[]{:S(2)}) %all-to-all-start.2) | async-done | bytes 1048608 | tf_op jit(solution)/shard_map/all_to_all | solution.py:55
  107.0 7.5 %reshape.193 = bf16[2048,2,8,16]{3,2,1,0:T(8,128)(2,1)} reshape(bf16[8,2,32768]{2,1,0:T(2,128)(2,1)S(1)} %all-to-all-done.2) | data formatting | bytes 2097152
  114.6 8.9 %copy.84 = bf16[2,16,8,8,256]{4,2,3,1,0:T(8,128)(2,1)S(1)} copy(bf16[2,16,8,8,256]{1,2,0,4,3:T(8,128)(2,1)} %bitcast.181) | data formatting | bytes 2097152 | tf_op jit(solution)/shard_map/all_to_all | solution.py:55
  125.3 43.3 %all-reduce.1 = bf16[1024,160]{0,1:T(8,128)(2,1)} all-reduce(f32[1024,160]{0,1:T(8,128)S(1)} %fusion.37), channel_id=1, replica_groups=mesh['req'=8,'grp'=4] {'req'}, use_global_device_ids=true, to_apply=%region_1.2 | all-reduce | flops 163840 | bytes 983040 | tf_op jit(solution)/shard_map/psum | solution.py:72
  169.6 2.7 compare_select_fusion
  172.3 2.4 reshape.153
  176.0 129.5 %while.15 = (s32[]{:T(128)}, f32[16,16384]{1,0:T(8,128)S(1)}, f32[16,16384]{1,0:T(8,128)S(1)}, f32[16,16384]{1,0:T(8,128)}, f32[16,16384]{1,0:T(8,128)}, /*index...) while((s32[]{:T(128)}, f32[16,16384]{1,0:T(8,128)S(1)}, ...), condition=%wide.region_4.5_spmd.clone, body=%wide.region_2.4_spmd.clone.sunk | while | flops 1835075 | bytes 18522668 | solution.py:109
  182.1 2.0 dynamic_update_slice.6
  190.2 2.0 dynamic_update_slice.6
  198.3 2.0 dynamic_update_slice.6
  206.4 2.0 dynamic_update_slice.6
  214.6 2.0 dynamic_update_slice.6
  218.2 1.3 constant_dynamic-slice_fusion.6
  222.7 2.0 dynamic_update_slice.6
  226.3 1.3 constant_dynamic-slice_fusion.6
  230.8 2.0 dynamic_update_slice.6
  234.4 1.3 constant_dynamic-slice_fusion.6
  238.9 2.0 dynamic_update_slice.6
  242.5 1.3 constant_dynamic-slice_fusion.6
  247.0 1.9 dynamic_update_slice.6
  250.6 1.3 constant_dynamic-slice_fusion.6
  255.1 1.9 dynamic_update_slice.6
  263.1 1.9 dynamic_update_slice.6
  271.2 1.9 dynamic_update_slice.6
  279.3 1.9 dynamic_update_slice.6
  287.4 1.9 dynamic_update_slice.6
  295.4 1.9 dynamic_update_slice.6
  303.5 1.9 dynamic_update_slice.6
  305.5 1.5 copy.105
  307.0 1.5 fusion.16
  309.6 3.5 %all-to-all-start.3 = ((bf16[16,64,256]{2,0,1:T(8,128)(2,1)}), bf16[16,64,256]{2,0,1:T(8,128)(2,1)S(1)}, u32[]{:S(2)}, u32[]{:S(2)}) async-start(bf16[16,64,256]{2,0,1:T(8,128)(2,1)} %copy.88), calls=%async_computation.3 | async-start | bytes 1048576 | tf_op jit(solution)/shard_map/all_to_all | solution.py:114
  314.2 9.2 %all-to-all-done.3 = bf16[16,64,256]{2,0,1:T(8,128)(2,1)S(1)} async-done(((bf16[16,64,256]{2,0,1:T(8,128)(2,1)}), bf16[16,64,256]{2,0,1:T(8,128)(2,1)S(1)}, u32[]{:S(2)}, u32[]{:S(2)}) %all-to-all-start.3) | async-done | bytes 524320 | tf_op jit(solution)/shard_map/all_to_all | solution.py:114
  323.4 3.8 %all-to-all-start.4 = ((f32[16,64,256]{2,0,1:T(8,128)}), f32[16,64,256]{2,0,1:T(8,128)S(1)}, u32[]{:S(2)}, u32[]{:S(2)}) async-start(f32[16,64,256]{2,0,1:T(8,128)} %bitcast.147), calls=%async_computation.4 | async-start | bytes 2097152 | tf_op jit(solution)/shard_map/all_to_all | solution.py:121
  327.6 3.0 fusion.2
  331.5 14.4 %all-to-all-done.4 = f32[16,64,256]{2,0,1:T(8,128)S(1)} async-done(((f32[16,64,256]{2,0,1:T(8,128)}), f32[16,64,256]{2,0,1:T(8,128)S(1)}, u32[]{:S(2)}, u32[]{:S(2)}) %all-to-all-start.4) | async-done | bytes 1048608 | tf_op jit(solution)/shard_map/all_to_all | solution.py:121
  346.4 1.6 copy.93
  (302 shorter events, 99.0 us)
Async XLA Ops:
  0.6 124.3 %copy-start = (bf16[256,160]{0,1:T(8,128)(2,1)S(1)}, bf16[256,160]{0,1:T(8,128)(2,1)}, u32[]{:S(2)}) copy-start(bf16[256,160]{0,1:T(8,128)(2,1)} %param.24) | copy-start | bytes 245764
  8.5 12.5 %copy-start.13 = (s32[64]{0:T(128)S(1)}, s32[64]{0:T(128)}, u32[]{:S(2)}) copy-start(s32[64]{0:T(128)} %param.33) | copy-start | bytes 772
  8.5 12.5 %copy-start.4 = (f32[8,16,2048]{2,1,0:T(8,128)S(1)}, f32[8,16,2048]{2,1,0:T(8,128)}, u32[]{:S(2)}) copy-start(f32[8,16,2048]{2,1,0:T(8,128)} %param.30) | copy-start | bytes 3145732
  8.5 17.2 %copy-start.14 = (s32[64]{0:T(128)S(1)}, s32[64]{0:T(128)}, u32[]{:S(2)}) copy-start(s32[64]{0:T(128)} %param.32) | copy-start | bytes 772
  8.5 17.4 %copy-start.3 = (bf16[8,16,1024]{2,1,0:T(8,128)(2,1)S(1)}, bf16[8,16,1024]{2,1,0:T(8,128)(2,1)}, u32[]{:S(2)}) copy-start(bf16[8,16,1024]{2,1,0:T(8,128)(2,1)} %param.19) | copy-start | bytes 786436
  8.5 17.7 %copy-start.5 = (f32[1024]{0:T(1024)S(1)}, f32[1024]{0:T(1024)}, u32[]{:S(2)}) copy-start(f32[1024]{0:T(1024)} %param.20) | copy-start | bytes 12292
  13.7 27.0 %all-to-all-start.1 = ((f32[8,1,6144]{2,1,0:T(1,128)}), f32[8,1,6144]{2,1,0:T(1,128)S(1)}, u32[]{:S(2)}, u32[]{:S(2)}) async-start(f32[8,1,6144]{2,1,0:T(1,128)} %reshape.194), calls=%async_computation.1 | async-start | bytes 393216 | tf_op jit(solution)/shard_map/all_to_all | solution.py:49
  26.2 4.8 %copy-start.10 = (s32[64]{0:T(128)S(1)}, s32[64]{0:T(128)}, u32[]{:S(2)}) copy-start(s32[64]{0:T(128)} %param.35) | copy-start | bytes 772
  40.7 35.4 %all-to-all-start = ((f32[8,16,8,256]{3,1,2,0:T(8,128)}), f32[8,16,8,256]{3,1,2,0:T(8,128)S(1)}, u32[]{:S(2)}, u32[]{:S(2)}) async-start(f32[8,16,8,256]{3,1,2,0:T(8,128)} %fusion.27), calls=%async_computation | async-start | bytes 2097152 | tf_op jit(solution)/shard_map/all_to_all | solution.py:44
  54.2 11.3 %copy-start.7 = (f32[4,256]{1,0:T(4,128)S(1)}, f32[4,256]{1,0:T(4,128)}, u32[]{:S(2)}) copy-start(f32[4,256]{1,0:T(4,128)} %param.22) | copy-start | bytes 12292
  54.2 11.3 %copy-start.6 = (f32[16,256]{1,0:T(8,128)S(1)}, f32[16,256]{1,0:T(8,128)}, u32[]{:S(2)}) copy-start(f32[16,256]{1,0:T(8,128)} %param.27) | copy-start | bytes 49156
  76.2 30.9 %all-to-all-start.2 = ((bf16[8,2,32768]{2,1,0:T(2,128)(2,1)}), bf16[8,2,32768]{2,1,0:T(2,128)(2,1)S(1)}, u32[]{:S(2)}, u32[]{:S(2)}) async-start(bf16[8,2,32768]{2,1,0:T(2,128)(2,1)} %reshape.192), calls=%async_computation.2 | async-start | bytes 2097152 | tf_op jit(solution)/shard_map/all_to_all | solution.py:55
  114.6 9.9 %copy-start.8 = (f32[256]{0:T(256)S(1)}, f32[256]{0:T(256)}, u32[]{:S(2)}) copy-start(f32[256]{0:T(256)} %param.23) | copy-start | bytes 3076
  123.5 1.0 copy-start.2
  123.5 46.1 %copy-start.11 = (bf16[128,256]{1,0:T(8,128)(2,1)S(1)}, bf16[128,256]{1,0:T(8,128)(2,1)}, u32[]{:S(2)}) copy-start(bf16[128,256]{1,0:T(8,128)(2,1)} %param.25) | copy-start | bytes 196612
  123.5 46.1 %copy-start.12 = (f32[256]{0:T(256)S(1)}, f32[256]{0:T(256)}, u32[]{:S(2)}) copy-start(f32[256]{0:T(256)} %param.26) | copy-start | bytes 3076
  125.3 50.7 %copy-start.15 = (s32[64]{0:T(128)S(1)}, s32[64]{0:T(128)}, u32[]{:S(2)}) copy-start(s32[64]{0:T(128)} %param.34) | copy-start | bytes 772
  176.0 131.0 %copy-start.9 = (f32[256]{0:T(256)S(1)}, f32[256]{0:T(256)}, u32[]{:S(2)}) copy-start(f32[256]{0:T(256)} %param.28) | copy-start | bytes 3076
  309.6 13.8 %all-to-all-start.3 = ((bf16[16,64,256]{2,0,1:T(8,128)(2,1)}), bf16[16,64,256]{2,0,1:T(8,128)(2,1)S(1)}, u32[]{:S(2)}, u32[]{:S(2)}) async-start(bf16[16,64,256]{2,0,1:T(8,128)(2,1)} %copy.88), calls=%async_computation.3 | async-start | bytes 1048576 | tf_op jit(solution)/shard_map/all_to_all | solution.py:114
  323.4 22.4 %all-to-all-start.4 = ((f32[16,64,256]{2,0,1:T(8,128)}), f32[16,64,256]{2,0,1:T(8,128)S(1)}, u32[]{:S(2)}, u32[]{:S(2)}) async-start(f32[16,64,256]{2,0,1:T(8,128)} %bitcast.147), calls=%async_computation.4 | async-start | bytes 2097152 | tf_op jit(solution)/shard_map/all_to_all | solution.py:121
  327.6 20.4 %copy-start.1 = (bf16[256,160]{0,1:T(8,128)(2,1)S(1)}, bf16[256,160]{0,1:T(8,128)(2,1)}, u32[]{:S(2)}) copy-start(bf16[256,160]{0,1:T(8,128)(2,1)} %param.24) | copy-start | bytes 245764
